TPU v7x, 32 devices: a whole 2x2x4 slice. The times are simulated.
32 devices in a mesh: section: 4 (over z), dp: 4 (over y, x), hid: 2 (over core).
Axes of the slice: x: 2, y: 2, z: 4, core: 2. Of those that a mesh axis runs over, the one named last changes fastest.
Arguments:
- forward_input: bfloat16 [4, 768, 2048], P('section', 'dp'), may hold values from -6 to 6
- backward_input: bfloat16 [4, 768, 2048], P('section', 'dp'), may hold values from -6 to 6
- output_grad: bfloat16 [4, 768, 2048], P('section', 'dp'), may hold values from -8 to 8
- norm_gain: float32 [4, 2048], P('section'), may hold values from 0.5 to 1.5
- in_weight: float32 [4, 2, 2048, 512], P('section', None, 'dp', 'hid'), may hold values from -0.125 to 0.125
- out_weight: float32 [4, 512, 2048], P('section', 'hid', 'dp'), may hold values from -0.25 to 0.25
- in_codes: int32 [4, 2, 2048, 512], P('section', None, 'dp', 'hid'), may hold values from 0 to 32511
- out_codes: int32 [4, 512, 2048], P('section', 'hid', 'dp'), may hold values from 0 to 32511
- in_scales: float32 [4, 2, 2, 2048, 2], P('section', None, None, 'dp', 'hid'), may hold values from 0.005 to 0.05
- out_scales: float32 [4, 2, 2, 2048], P('section', None, 'hid', 'dp'), may hold values from 0.005 to 0.05
- section_lags: int32 [4], P('section'), may hold values from 1 to 4
Outputs:
- next_input: bfloat16 [4, 768, 2048], P('section', 'dp')
- input_grad: bfloat16 [4, 768, 2048], P('section', 'dp')
- in_update: float32 [4, 2, 2048, 512], P('section', None, 'dp', 'hid')
- out_update: float32 [4, 512, 2048], P('section', 'hid', 'dp')
Inputs may be any that keep to these rules, and one draw needn't show every extreme that they name: `in_codes`: each code holds a first-moment code of 0 to 126 times 256 plus a second-moment code of 0 to 255. `out_codes`: each code holds a first-moment code of 0 to 126 times 256 plus a second-moment code of 0 to 255.
All inputs are finite; a program needn't handle non-finite values.
Results may differ from a plain program's by a relative error of at most 0.012.
Values may be sent and summed in bfloat16 or wider, within the bound.
A program may use at most 64 MiB of HBM per device.

v0:
```python
import jax
import jax.numpy as jnp
from jax import lax
from jax.sharding import PartitionSpec as P

QB = 256
STEP = 1000
BETA_ONE = 0.9
BETA_TWO = 0.999
ADAM_EPS = 1e-08
NORM_EPS = 1e-06
LEARN_RATE = 0.003


def passed_along(block, axis, distance):
    devices = range(lax.axis_size(axis))
    route = [(i - distance, i) for i in devices if i - distance in devices]
    return lax.ppermute(block, axis, route)


def dequant(codes, first_scale, second_scale):
    high = (codes // 256).astype(jnp.float32)
    low = (codes % 256).astype(jnp.float32)
    moment_m = first_scale * (high - 63.0) / 63.0
    moment_v = jnp.square(second_scale * (0.25 + 0.75 * low / 255.0))
    return (moment_m, moment_v)


def direction(moment_m, moment_v, count):
    return (
        moment_m
        / (1.0 - BETA_ONE**count)
        / (jnp.sqrt(moment_v / (1.0 - BETA_TWO**count)) + ADAM_EPS)
    )


def normalize(inputs, gain):
    values = inputs.astype(jnp.float32)
    factor = lax.rsqrt(jnp.mean(values * values, axis=-1, keepdims=True) + NORM_EPS)
    return ((values * factor * gain).astype(jnp.bfloat16), factor, values)


def local(
    forward_input,
    backward_input,
    output_grad,
    norm_gain,
    in_weight,
    out_weight,
    in_codes,
    out_codes,
    in_scales,
    out_scales,
    section_lags,
):
    lag_value = section_lags[0].astype(jnp.float32)
    gain = norm_gain[0]
    m_in, v_in = dequant(
        in_codes[0],
        jnp.repeat(in_scales[0, 0], QB, axis=-1),
        jnp.repeat(in_scales[0, 1], QB, axis=-1),
    )
    m_out, v_out = dequant(
        out_codes[0],
        jnp.repeat(out_scales[0, 0], QB, axis=0),
        jnp.repeat(out_scales[0, 1], QB, axis=0),
    )
    pred_in = (in_weight[0] - LEARN_RATE * lag_value * direction(m_in, v_in, STEP - 1)).astype(
        jnp.bfloat16
    )
    pred_out = (out_weight[0] - LEARN_RATE * lag_value * direction(m_out, v_out, STEP - 1)).astype(
        jnp.bfloat16
    )
    full_in, full_out = (
        lax.all_gather(pred_in, "dp", axis=1, tiled=True),
        lax.all_gather(pred_out, "dp", axis=1, tiled=True),
    )
    normed, factor, values = normalize(forward_input[0], gain)
    gate_val = jnp.dot(normed, full_in[0], preferred_element_type=jnp.float32)
    up_val = jnp.dot(normed, full_in[1], preferred_element_type=jnp.float32)
    hidden = (gate_val * jax.nn.sigmoid(gate_val) * up_val).astype(jnp.bfloat16)
    partial_value = jnp.dot(hidden, full_out, preferred_element_type=jnp.float32)
    back_in, back_out = (full_in, full_out)
    out_cot = output_grad[0]
    normed_b, factor_b, values_b = normalize(backward_input[0], gain)
    gate_b = jnp.dot(normed_b, back_in[0], preferred_element_type=jnp.float32)
    up_b = jnp.dot(normed_b, back_in[1], preferred_element_type=jnp.float32)
    sig_b = jax.nn.sigmoid(gate_b)
    hidden_b = (gate_b * sig_b * up_b).astype(jnp.bfloat16)
    grad_h = jnp.dot(out_cot, back_out.T, preferred_element_type=jnp.float32)
    grad_gate = (grad_h * up_b * sig_b * (1.0 + gate_b * (1.0 - sig_b))).astype(jnp.bfloat16)
    grad_up = (grad_h * gate_b * sig_b).astype(jnp.bfloat16)
    grad_part = jnp.dot(grad_gate, back_in[0].T, preferred_element_type=jnp.float32) + jnp.dot(
        grad_up, back_in[1].T, preferred_element_type=jnp.float32
    )
    summed, grad_n = (
        lax.psum(partial_value.astype(jnp.bfloat16), "hid").astype(jnp.float32),
        lax.psum(grad_part.astype(jnp.bfloat16), "hid").astype(jnp.float32),
    )
    ahead = (values + summed).astype(jnp.bfloat16)
    next_rows = passed_along(ahead, "section", 1)
    scaled = gain * grad_n
    grad_x = (
        out_cot.astype(jnp.float32)
        + factor_b * scaled
        - values_b * factor_b**3 * jnp.mean(scaled * values_b, axis=-1, keepdims=True)
    )
    back_rows = passed_along(grad_x.astype(jnp.bfloat16), "section", -1)
    local_in = jnp.stack(
        [
            jnp.dot(normed_b.T, grad_gate, preferred_element_type=jnp.float32),
            jnp.dot(normed_b.T, grad_up, preferred_element_type=jnp.float32),
        ]
    )
    local_out = jnp.dot(hidden_b.T, out_cot, preferred_element_type=jnp.float32)
    sum_in, sum_out = (
        lax.psum_scatter(
            local_in.astype(jnp.bfloat16), "dp", scatter_dimension=1, tiled=True
        ).astype(jnp.float32),
        lax.psum_scatter(
            local_out.astype(jnp.bfloat16), "dp", scatter_dimension=1, tiled=True
        ).astype(jnp.float32),
    )
    rows_all = out_cot.shape[0] * lax.axis_size("dp")
    grad_in = sum_in / rows_all
    grad_out = sum_out / rows_all
    new_m_in = BETA_ONE * m_in + (1.0 - BETA_ONE) * grad_in
    new_v_in = BETA_TWO * v_in + (1.0 - BETA_TWO) * grad_in * grad_in
    new_m_out = BETA_ONE * m_out + (1.0 - BETA_ONE) * grad_out
    new_v_out = BETA_TWO * v_out + (1.0 - BETA_TWO) * grad_out * grad_out
    in_update = direction(new_m_in, new_v_in, STEP)
    out_update = direction(new_m_out, new_v_out, STEP)
    return (next_rows[None], back_rows[None], in_update[None], out_update[None])


def solution(mesh):
    in_specs = (
        P("section", "dp", None),
        P("section", "dp", None),
        P("section", "dp", None),
        P("section", None),
        P("section", None, "dp", "hid"),
        P("section", "hid", "dp"),
        P("section", None, "dp", "hid"),
        P("section", "hid", "dp"),
        P("section", None, None, "dp", "hid"),
        P("section", None, "hid", "dp"),
        P("section"),
    )
    out_specs = (
        P("section", "dp", None),
        P("section", "dp", None),
        P("section", None, "dp", "hid"),
        P("section", "hid", "dp"),
    )
    return jax.shard_map(local, mesh=mesh, in_specs=in_specs, out_specs=out_specs, check_vma=False)
```

profile of v0, /device:TPU:0, one launch (start us, length us, event | category | flops | bytes accessed | tf_op | source)
XLA Modules:
  0.0 193.6 jit_solution(17537712004479626247)
XLA Ops:
  7.2 0.0 all-gather.3.cloned.1.call-start
  7.9 0.7 fusion.87
  8.6 0.0 copy-start.13
  8.6 4.1 %fusion.40 = bf16[2,512,256]{2,1,0:T(8,128)(2,1)} fusion(f32[1,2,512,256]{3,2,1,0:T(8,128)} %param.15, f32[]{:T(128)} %bitcast.4, s32[1,2,512,256]{3,2,1,0:T(8,128)} %param.17, f32[2,512]{1,0:T(2,128)S(1)} %get-tuple-element.17, f32[2,512]{1,0:T(2,128)S(1)} %get-tuple-element.16), kind=kLoop, calls=%fused_computation.66 | loop fusion | flops 8912896 | bytes 2629636 | tf_op jit(solution)/shard_map/convert_element_type | solution.py:68
  12.7 0.0 all-gather.3.cloned.1.call-update
  12.7 0.0 reduce-scatter.5.cloned.1.call-start
  12.8 0.2 fusion.13
  13.0 37.7 %all-gather.3.cloned.1.call-done = bf16[2,2048,256]{2,1,0:T(8,128)(2,1)} async-done(((bf16[2,512,256]{2,1,0:T(8,128)(2,1)}), bf16[2,2048,256]{2,1,0:T(8,128)(2,1)}) %all-gather.3.cloned.1.call-update) | async-done | bytes 2097168 | tf_op jit(solution)/shard_map/all_gather | solution.py:75
  50.8 0.0 copy-done.13
  50.8 1.8 fusion.45
  52.6 0.1 copy-done.5
  52.7 0.4 fusion.43
  53.1 0.8 copy-done.3
  53.9 1.5 convolution_convert_fusion
  55.4 0.0 copy-done.9
  55.4 0.0 reduce-scatter.5.cloned.1.call-update
  55.4 0.0 all-gather.5.cloned.1.call-start
  55.5 28.0 %reduce-scatter.5.cloned.1.call-done = bf16[256,512]{1,0:T(8,128)(2,1)} async-done(((bf16[256,2048]{1,0:T(8,128)(2,1)}), bf16[256,512]{1,0:T(8,128)(2,1)}) %reduce-scatter.5.cloned.1.call-update) | async-done | bytes 262160 | tf_op jit(solution)/shard_map/reduce_scatter | solution.py:120
  83.5 3.0 %fusion.61 = (f32[1,256,512]{2,1,0:T(8,128)}, bf16[256,512]{1,0:T(8,128)(2,1)}) fusion(bf16[256,512]{1,0:T(8,128)(2,1)} %reduce-scatter.5.cloned.1.call-done, s32[1,256,512]{2,1,0:T(8,128)S(1)} %copy-done.7, f32[512]{0:T(512)S(1)} %bitcast.177, f32[512]{0:T(512)S(1)} %bitcast.176, f32[]{:T(128)} %bitcast.4, f32[1,256,512]{2,1,0:T(8,128)S(1)} %copy-done.8), kind=kLoop, calls=%fused_computation.95 | loop fusion | flops 6029312 | bytes 2101252 | tf_op jit(solution)/shard_map/broadcast_in_dim | solution.py:133
  86.5 0.0 all-gather.5.cloned.1.call-update
  86.5 0.0 all-reduce.3.cloned.1.call-start
  86.6 0.2 fusion.9
  86.8 0.0 copy-start.12
  86.8 1.7 fusion.44
  88.6 24.5 %all-gather.5.cloned.1.call-done = bf16[256,2048]{1,0:T(8,128)(2,1)} async-done(((bf16[256,512]{1,0:T(8,128)(2,1)}), bf16[256,2048]{1,0:T(8,128)(2,1)}) %all-gather.5.cloned.1.call-update) | async-done | bytes 1048592 | tf_op jit(solution)/shard_map/all_gather | solution.py:76
  113.0 1.7 multiply_convert_fusion.1
  114.8 3.5 %convolution_convert_fusion.3 = bf16[192,2048]{1,0:T(8,128)(2,1)} fusion(bf16[256,2048]{1,0:T(8,128)(2,1)} %all-gather.5.cloned.1.call-done, bf16[2,2048,256]{2,1,0:T(8,128)(2,1)} %all-gather.3.cloned.1.call-done, bf16[1,192,2048]{2,1,0:T(8,128)(2,1)S(1)} %copy-done.2, f32[2048]{0:T(1024)S(1)} %bitcast.171, f32[192]{0:T(256)S(1)} %add_rsqrt_fusion.1, ...), kind=kOutput, calls=%fused_computation.5 | convolution fusion | flops 404914176 | bytes 3875584 | tf_op jit(solution)/shard_map/dot_general | solution.py:82
  118.3 1.9 fusion.42
  120.2 0.0 copy-done.6
  120.2 1.4 fusion
  121.6 0.0 all-reduce.3.cloned.1.call-update
  121.6 0.0 reduce-scatter.3.cloned.1.call-start
  121.7 0.6 fusion.2
  122.3 0.6 fusion.1
  122.8 1.5 pad_maximum_fusion
  124.3 0.0 reduce-scatter.3.cloned.1.call-update
  124.4 17.8 %all-reduce.3.cloned.1.call-done = (bf16[192,2048]{1,0:T(8,128)(2,1)}, bf16[192,2048]{1,0:T(8,128)(2,1)}) async-done(((bf16[192,2048]{1,0:T(8,128)(2,1)}, bf16[192,2048]{1,0:T(8,128)(2,1)}), (bf16[192,2048]{1,0:T(8,128)(2,1)}, bf16[192,2048]{1,0:T(8,128)(2,1)})) %all-reduce.3.cloned.1.call-update) | async-done | bytes 1572880 | tf_op jit(solution)/shard_map/psum | solution.py:97
  142.2 1.5 fusion.10
  143.7 3.7 %collective-permute-start = (bf16[192,2048]{1,0:T(8,128)(2,1)S(1)}, bf16[192,2048]{1,0:T(8,128)(2,1)S(1)}, u32[]{:S(2)}, u32[]{:S(2)}) collective-permute-start(bf16[192,2048]{1,0:T(8,128)(2,1)S(1)} %fusion.10), channel_id=1, source_target_pairs={{0,8},{8,16},{16,24},{1,9},{9,17},{17,25},{2,10},{10,18},{18,26},{... | collective-permute-start | bytes 2359304 | tf_op jit(solution)/shard_map/ppermute | solution.py:18
  147.4 0.3 fusion.17
  147.8 0.6 fusion.16
  148.4 1.3 collective-permute-start.1
  149.7 14.9 %collective-permute-done = bf16[192,2048]{1,0:T(8,128)(2,1)S(1)} collective-permute-done((bf16[192,2048]{1,0:T(8,128)(2,1)S(1)}, bf16[192,2048]{1,0:T(8,128)(2,1)S(1)}, u32[]{:S(2)}, u32[]{:S(2)}) %collective-permute-start) | collective-permute-done | bytes 786464 | tf_op jit(solution)/shard_map/ppermute | solution.py:18
  164.6 5.1 %collective-permute-done.1 = bf16[192,2048]{1,0:T(8,128)(2,1)S(1)} collective-permute-done((bf16[192,2048]{1,0:T(8,128)(2,1)S(1)}, bf16[192,2048]{1,0:T(8,128)(2,1)S(1)}, u32[]{:S(2)}, u32[]{:S(2)}) %collective-permute-start.1) | collective-permute-done | bytes 786464 | tf_op jit(solution)/shard_map/ppermute | solution.py:18
  169.7 11.7 %reduce-scatter.3.cloned.1.call-done = bf16[2,512,256]{2,1,0:T(8,128)(2,1)} async-done(((bf16[2,2048,256]{2,1,0:T(8,128)(2,1)}), bf16[2,512,256]{2,1,0:T(8,128)(2,1)}) %reduce-scatter.3.cloned.1.call-update) | async-done | bytes 524304 | tf_op jit(solution)/shard_map/reduce_scatter | solution.py:117
  181.4 3.9 %fusion.33 = f32[1,2,512,256]{3,2,1,0:T(8,128)} fusion(bf16[2,512,256]{2,1,0:T(8,128)(2,1)} %reduce-scatter.3.cloned.1.call-done, s32[1,2,512,256]{3,2,1,0:T(8,128)S(1)} %copy-done.1, f32[2,512]{1,0:T(2,128)S(1)} %get-tuple-element.17, f32[2,512]{1,0:T(2,128)S(1)} %get-tuple-element.16), kind=kLoop, calls=%fused_computation.54 | loop fusion | flops 10223616 | bytes 2629632 | tf_op jit(solution)/shard_map/broadcast_in_dim | solution.py:133
  185.3 0.9 copy.24
  186.2 0.9 copy.25
  (28 shorter events, 0.1 us)
Async XLA Ops:
  7.2 43.6 %all-gather.3.cloned.1.call-start = ((), (), s32[]{:S(2)}) async-start(), calls=%async_computation.2 | async-start | bytes 2621440 | tf_op jit(solution)/shard_map/all_gather | solution.py:75
  8.6 4.2 %copy-start = (bf16[1,192,2048]{2,1,0:T(8,128)(2,1)S(1)}, bf16[1,192,2048]{2,1,0:T(8,128)(2,1)}, u32[]{:S(2)}) copy-start(bf16[1,192,2048]{2,1,0:T(8,128)(2,1)} %param.12) | copy-start | bytes 2359300
  8.6 42.2 %copy-start.13 = (f32[1,2048]{1,0:T(1,128)S(1)}, f32[1,2048]{1,0:T(1,128)}, u32[]{:S(2)}) copy-start(f32[1,2048]{1,0:T(1,128)} %param.14) | copy-start | bytes 24580
  12.7 70.8 %reduce-scatter.5.cloned.1.call-start = ((), (), s32[]{:S(2)}) async-start(), calls=%async_computation.5 | async-start | bytes 1310720 | tf_op jit(solution)/shard_map/reduce_scatter | solution.py:120
  50.8 1.9 copy-start.5
  52.7 2.7 %copy-start.9 = (f32[192,256]{1,0:T(8,128)}, f32[192,256]{1,0:T(8,128)S(1)}, u32[]{:S(2)}) copy-start(f32[192,256]{1,0:T(8,128)S(1)} %fusion.45) | copy-start | bytes 589828
  52.7 1.2 copy-start.3
  53.9 1.5 copy-start.11
  53.9 1.6 copy-start.14
  53.9 29.6 %copy-start.7 = (s32[1,256,512]{2,1,0:T(8,128)S(1)}, s32[1,256,512]{2,1,0:T(8,128)}, u32[]{:S(2)}) copy-start(s32[1,256,512]{2,1,0:T(8,128)} %param.18) | copy-start | bytes 1572868
  53.9 29.6 %copy-start.8 = (f32[1,256,512]{2,1,0:T(8,128)S(1)}, f32[1,256,512]{2,1,0:T(8,128)}, u32[]{:S(2)}) copy-start(f32[1,256,512]{2,1,0:T(8,128)} %param.16) | copy-start | bytes 1572868
  55.4 31.2 %copy-start.2 = (bf16[1,192,2048]{2,1,0:T(8,128)(2,1)S(1)}, bf16[1,192,2048]{2,1,0:T(8,128)(2,1)}, u32[]{:S(2)}) copy-start(bf16[1,192,2048]{2,1,0:T(8,128)(2,1)} %param.11) | copy-start | bytes 2359300
  55.4 57.6 %all-gather.5.cloned.1.call-start = ((), (), s32[]{:S(2)}) async-start(), calls=%async_computation.3 | async-start | bytes 1310720 | tf_op jit(solution)/shard_map/all_gather | solution.py:76
  86.5 55.7 %all-reduce.3.cloned.1.call-start = ((), (), s32[]{:S(2)}) async-start(), calls=%async_computation.6 | async-start | bytes 3145728 | tf_op jit(solution)/shard_map/psum | solution.py:97
  86.8 26.2 %copy-start.10 = (f32[192,256]{1,0:T(8,128)S(1)}, f32[192,256]{1,0:T(8,128)}, u32[]{:S(2)}) copy-start(f32[192,256]{1,0:T(8,128)} %copy-done.9) | copy-start | bytes 589828
  86.8 26.2 %copy-start.12 = (f32[192,256]{1,0:T(8,128)S(1)}, f32[192,256]{1,0:T(8,128)}, u32[]{:S(2)}) copy-start(f32[192,256]{1,0:T(8,128)} %copy-done.11) | copy-start | bytes 589828
  118.3 1.9 copy-start.6
  121.6 59.8 %reduce-scatter.3.cloned.1.call-start = ((), (), s32[]{:S(2)}) async-start(), calls=%async_computation.4 | async-start | bytes 2621440 | tf_op jit(solution)/shard_map/reduce_scatter | solution.py:117
  142.2 5.2 %copy-start.4 = (bf16[192,2048]{1,0:T(8,128)(2,1)S(1)}, bf16[192,2048]{1,0:T(8,128)(2,1)}, u32[]{:S(2)}) copy-start(bf16[192,2048]{1,0:T(8,128)(2,1)} %get-tuple-element.5) | copy-start | bytes 2359300
  143.7 20.9 %collective-permute-start = (bf16[192,2048]{1,0:T(8,128)(2,1)S(1)}, bf16[192,2048]{1,0:T(8,128)(2,1)S(1)}, u32[]{:S(2)}, u32[]{:S(2)}) collective-permute-start(bf16[192,2048]{1,0:T(8,128)(2,1)S(1)} %fusion.10), channel_id=1, source_target_pairs={{0,8},{8,16},{16,24},{1,9},{9,17},{17,25},{2,10},{10,18},{18,26},{... | collective-permute-start | bytes 2359304 | tf_op jit(solution)/shard_map/ppermute | solution.py:18
  147.8 33.6 %copy-start.1 = (s32[1,2,512,256]{3,2,1,0:T(8,128)S(1)}, s32[1,2,512,256]{3,2,1,0:T(8,128)}, u32[]{:S(2)}) copy-start(s32[1,2,512,256]{3,2,1,0:T(8,128)} %param.17) | copy-start | bytes 3145732
  148.4 21.3 %collective-permute-start.1 = (bf16[192,2048]{1,0:T(8,128)(2,1)S(1)}, bf16[192,2048]{1,0:T(8,128)(2,1)S(1)}, u32[]{:S(2)}, u32[]{:S(2)}) collective-permute-start(bf16[192,2048]{1,0:T(8,128)(2,1)S(1)} %fusion.16), channel_id=1, source_target_pairs={{8,0},{16,8},{24,16},{9,1},{17,9},{25,17},{10,2},{18,10},{26,18},{... | collective-permute-start | bytes 2359304 | tf_op jit(solution)/shard_map/ppermute | solution.py:18
Sparse Core Ops, SparseCore 0:
  12.8 37.8 all-gather.2
  55.5 27.9 reduce-scatter.4
  86.6 26.3 all-gather.4
  121.7 20.4 all-reduce.2
  145.0 36.3 reduce-scatter.2
where the time goes:
time: 194 us
  waiting for transfers between devices  140 us (72%)
  other arithmetic  15.4 us (8%)
  matrix products  15.1 us (8%)
  between operations  14.6 us (8%)
  starting transfers between devices  5.21 us (3%)
  local copies, waits for them, and re-layouts  3.42 us (2%)
    all_gather x1, waiting for transfers between devices, local(): lax.all_gather(pred_in, 'dp', axis=1, tiled=True)  37.7 us
    reduce_scatter x1, waiting for transfers between devices, local(): lax.psum_scatter(local_out.astype(jnp.bfloat16), 'dp', scatter_dimension=...  28 us
    all_gather x1, waiting for transfers between devices, local(): lax.all_gather(pred_out, 'dp', axis=1, tiled=True)  24.5 us
    ppermute x2, waiting for transfers between devices, passed_along(): return lax.ppermute(block, axis, route)  20 us
    psum x1, waiting for transfers between devices, local(): lax.psum(partial_value.astype(jnp.bfloat16), 'hid').astype(jnp.float32)  17.8 us
    reduce_scatter x1, waiting for transfers between devices, local(): lax.psum_scatter(local_in.astype(jnp.bfloat16), 'dp', scatter_dimension=1...  11.7 us
    broadcast_in_dim x2, other arithmetic, local(): return (next_rows[None], back_rows[None], in_update[None], out_update[None])  6.92 us
    ppermute x2, starting transfers between devices, passed_along(): return lax.ppermute(block, axis, route)  5.01 us
  transfers between devices with their start and end apart: 7, of which 7 were waited for; matrix products, arithmetic and copies ran while one was open for 4% of the time, Pallas kernels for 0%

commit v1 on v0

--- a/solution.py
+++ b/solution.py
@@ -10,6 +10,11 @@
 ADAM_EPS = 1e-08
 NORM_EPS = 1e-06
 LEARN_RATE = 0.003
+
+
+def stack_and_merge(x, mesh_axis, dim):
+    parts = lax.all_gather(x, mesh_axis)
+    return jnp.concatenate(parts, axis=dim)
 
 
 def passed_along(block, axis, distance):
@@ -73,7 +78,7 @@
     )
     full_in, full_out = (
         lax.all_gather(pred_in, "dp", axis=1, tiled=True),
-        lax.all_gather(pred_out, "dp", axis=1, tiled=True),
+        stack_and_merge(pred_out, "dp", 1),
     )
     normed, factor, values = normalize(forward_input[0], gain)
     gate_val = jnp.dot(normed, full_in[0], preferred_element_type=jnp.float32)

time: 194 us -> 196 us (1.010)
  waiting for transfers between devices: 140 us -> 133 us
  local copies, waits for them, and re-layouts: 3.42 us -> 7.65 us
  other arithmetic: 15.4 us -> 19.3 us
    reduce_scatter x1, waiting for transfers between devices: 11.7 us -> 35.3 us  [local(): lax.psum_scatter(local_in.astype(jnp.bfloat16), 'dp', scatter_dimension=1...]
    ppermute x2, waiting for transfers between devices: 20 us -> 0.01 us  [passed_along(): return lax.ppermute(block, axis, route)]
    reduce_scatter x1, waiting for transfers between devices: 28 us -> 22.3 us  [local(): lax.psum_scatter(local_out.astype(jnp.bfloat16), 'dp', scatter_dimension=...]
    psum x1, waiting for transfers between devices: 17.8 us -> 15 us  [local(): lax.psum(partial_value.astype(jnp.bfloat16), 'hid').astype(jnp.float32)]
    convert_element_type x0 -> x1, other arithmetic: none -> 2.75 us  [local(): (out_weight[0] - LEARN_RATE * lag_value * direction(m_out, v_out, STEP -...]
    all_gather x1, waiting for transfers between devices: 37.7 us -> 35.4 us  [local(): lax.all_gather(pred_in, 'dp', axis=1, tiled=True)]
    all_gather x0 -> x1, local copies, waits for them, and re-layouts: none -> 2.26 us  [stack_and_merge(): parts = lax.all_gather(x, mesh_axis)]
    unnamed x33 -> x31, local copies, waits for them, and re-layouts: 2.71 us -> 4.61 us
  transfers between devices with their start and end apart: 7 -> 7, of which waited for: 7 -> 5; matrix products, arithmetic and copies ran while one was open for 4% -> 9% of each run, Pallas kernels for 0% -> 0%
where the time goes in v1:
time: 196 us
  waiting for transfers between devices  133 us (68%)
  other arithmetic  19.3 us (10%)
  matrix products  15 us (8%)
  between operations  14.6 us (7%)
  local copies, waits for them, and re-layouts  7.65 us (4%)
  starting transfers between devices  6.2 us (3%)
    all_gather x1, waiting for transfers between devices, local(): lax.all_gather(pred_in, 'dp', axis=1, tiled=True)  35.4 us
    reduce_scatter x1, waiting for transfers between devices, local(): lax.psum_scatter(local_in.astype(jnp.bfloat16), 'dp', scatter_dimension=1...  35.3 us
    all_gather x1, waiting for transfers between devices, stack_and_merge(): parts = lax.all_gather(x, mesh_axis)  24.8 us
    reduce_scatter x1, waiting for transfers between devices, local(): lax.psum_scatter(local_out.astype(jnp.bfloat16), 'dp', scatter_dimension=...  22.3 us
    psum x1, waiting for transfers between devices, local(): lax.psum(partial_value.astype(jnp.bfloat16), 'hid').astype(jnp.float32)  15 us
    broadcast_in_dim x2, other arithmetic, local(): return (next_rows[None], back_rows[None], in_update[None], out_update[None])  6.56 us
    ppermute x2, starting transfers between devices, passed_along(): return lax.ppermute(block, axis, route)  6 us
    unnamed x31, local copies, waits for them, and re-layouts  4.61 us
  transfers between devices with their start and end apart: 7, of which 5 were waited for; matrix products, arithmetic and copies ran while one was open for 9% of the time, Pallas kernels for 0%

profile of v1, /device:TPU:0, one launch (start us, length us, event | category | flops | bytes accessed | tf_op | source)
XLA Modules:
  0.0 195.6 jit_solution(12227045745335606454)
XLA Ops:
  7.2 0.0 all-gather.5.cloned.1.call-start
  7.2 0.8 fusion.108
  8.7 2.7 %subtract_convert_fusion = bf16[1,256,512]{2,1,0:T(8,128)(2,1)} fusion(f32[1,256,512]{2,1,0:T(8,128)} %param.16, s32[1,256,512]{2,1,0:T(8,128)} %param.18, f32[512]{0:T(512)S(1)} %bitcast.164, f32[512]{0:T(512)S(1)} %bitcast.162, f32[]{:T(128)} %bitcast.4), kind=kLoop, calls=%fused_computation.125 | loop fusion | flops 4456448 | bytes 1314820 | tf_op jit(solution)/shard_map/convert_element_type | solution.py:76
  11.4 0.0 all-gather.5.cloned.1.call-update
  11.4 0.0 all-gather.3.cloned.1.call-start
  11.5 0.0 copy-start.2
  11.5 0.0 copy-start
  11.6 3.8 %fusion.40 = bf16[2,512,256]{2,1,0:T(8,128)(2,1)} fusion(f32[1,2,512,256]{3,2,1,0:T(8,128)} %param.15, f32[]{:T(128)} %bitcast.4, s32[1,2,512,256]{3,2,1,0:T(8,128)S(1)} %copy-done.1, f32[2,512]{1,0:T(2,128)S(1)} %get-tuple-element.15, f32[2,512]{1,0:T(2,128)S(1)} %get-tuple-element.14), kind=kLoop, calls=%fused_computation.66 | loop fusion | flops 8912896 | bytes 2629636 | tf_op jit(solution)/shard_map/convert_element_type | solution.py:73
  15.4 0.0 all-gather.3.cloned.1.call-update
  15.4 0.0 all-reduce.3.cloned.1.call-start
  15.5 0.2 fusion.9
  15.7 0.2 fusion.13
  16.0 24.8 %all-gather.5.cloned.1.call-done = bf16[4,256,512]{2,1,0:T(8,128)(2,1)} async-done(((bf16[1,256,512]{2,1,0:T(8,128)(2,1)}), bf16[4,256,512]{2,1,0:T(8,128)(2,1)}) %all-gather.5.cloned.1.call-update) | async-done | bytes 1048592 | tf_op jit(solution)/shard_map/all_gather | solution.py:16
  40.8 2.3 %copy.20 = bf16[4,256,512]{1,2,0:T(8,128)(2,1)} copy(bf16[4,256,512]{2,1,0:T(8,128)(2,1)} %all-gather.5.cloned.1.call-done) | data formatting | bytes 2097152 | tf_op jit(solution)/shard_map/all_gather | solution.py:16
  43.1 35.4 %all-gather.3.cloned.1.call-done = bf16[2,2048,256]{2,1,0:T(8,128)(2,1)} async-done(((bf16[2,512,256]{2,1,0:T(8,128)(2,1)}), bf16[2,2048,256]{2,1,0:T(8,128)(2,1)}) %all-gather.3.cloned.1.call-update) | async-done | bytes 2097168 | tf_op jit(solution)/shard_map/all_gather | solution.py:80
  78.4 1.8 fusion.43
  80.3 0.1 copy-done.6
  80.4 0.4 fusion.45
  80.8 0.8 copy-done.3
  81.6 0.4 copy-done.8
  82.0 1.0 multiply_convert_fusion.1
  83.0 1.1 fusion.44
  84.1 3.7 %convolution_convert_fusion.3 = bf16[192,2048]{1,0:T(8,128)(2,1)} fusion(bf16[256,2048]{0,1:T(8,128)(2,1)} %bitcast.151, bf16[2,2048,256]{2,1,0:T(8,128)(2,1)} %all-gather.3.cloned.1.call-done, bf16[1,192,2048]{2,1,0:T(8,128)(2,1)S(1)} %copy-done.2, f32[2048]{0:T(1024)S(1)} %bitcast.157, f32[192]{0:T(256)S(1)} %add_rsqrt_fusion.1, f32[192,256]{1,0:T(8,128)} %fusion.44), kind=kOutput, calls=%fused_computation.5 | convolution fusion | flops 404914176 | bytes 3875584 | tf_op jit(solution)/shard_map/dot_general | solution.py:87
  87.8 1.9 fusion.42
  89.7 0.0 copy-done.7
  89.7 1.4 fusion
  91.1 0.0 all-reduce.3.cloned.1.call-update
  91.1 0.0 reduce-scatter.5.cloned.1.call-start
  91.2 2.5 %convolution_convert_fusion = bf16[256,2048]{1,0:T(8,128)(2,1)} fusion(bf16[1,192,2048]{2,1,0:T(8,128)(2,1)S(1)} %copy-done.3, f32[192,256]{1,0:T(8,128)} %copy-done.10, f32[192,256]{1,0:T(8,128)} %copy-done.9), kind=kOutput, calls=%fused_computation.1 | convolution fusion | flops 202145792 | bytes 2228224 | tf_op jit(solution)/shard_map/dot_general | solution.py:120
  93.7 0.0 reduce-scatter.5.cloned.1.call-update
  93.7 0.0 reduce-scatter.3.cloned.1.call-start
  93.7 0.6 fusion.2
  94.3 0.3 copy-done.11
  94.6 0.6 fusion.1
  95.2 1.5 pad_maximum_fusion
  96.7 0.0 reduce-scatter.3.cloned.1.call-update
  96.7 15.0 %all-reduce.3.cloned.1.call-done = (bf16[192,2048]{1,0:T(8,128)(2,1)}, bf16[192,2048]{1,0:T(8,128)(2,1)}) async-done(((bf16[192,2048]{1,0:T(8,128)(2,1)}, bf16[192,2048]{1,0:T(8,128)(2,1)}), (bf16[192,2048]{1,0:T(8,128)(2,1)}, bf16[192,2048]{1,0:T(8,128)(2,1)})) %all-reduce.3.cloned.1.call-update) | async-done | bytes 1572880 | tf_op jit(solution)/shard_map/psum | solution.py:102
  111.7 2.4 %fusion.10 = bf16[192,2048]{1,0:T(8,128)(2,1)} fusion(bf16[1,192,2048]{2,1,0:T(8,128)(2,1)S(1)} %copy-done.2, bf16[192,2048]{1,0:T(8,128)(2,1)} %get-tuple-element.4), kind=kLoop, calls=%fused_computation.20 | loop fusion | flops 1572864 | bytes 2359296 | tf_op jit(solution)/shard_map/convert_element_type | solution.py:105
  114.1 4.5 %collective-permute-start = (bf16[192,2048]{1,0:T(8,128)(2,1)}, bf16[192,2048]{1,0:T(8,128)(2,1)}, u32[]{:S(2)}, u32[]{:S(2)}) collective-permute-start(bf16[192,2048]{1,0:T(8,128)(2,1)} %fusion.10), channel_id=1, source_target_pairs={{0,8},{8,16},{16,24},{1,9},{9,17},{17,25},{2,10},{10,18},{18,26},{... | collective-permute-start | bytes 2359304 | tf_op jit(solution)/shard_map/ppermute | solution.py:23
  118.6 0.3 fusion.17
  119.0 1.5 fusion.16
  120.5 1.5 collective-permute-start.1
  121.9 22.3 %reduce-scatter.5.cloned.1.call-done = bf16[256,512]{1,0:T(8,128)(2,1)} async-done(((bf16[256,2048]{1,0:T(8,128)(2,1)}), bf16[256,512]{1,0:T(8,128)(2,1)}) %reduce-scatter.5.cloned.1.call-update) | async-done | bytes 262160 | tf_op jit(solution)/shard_map/reduce_scatter | solution.py:125
  144.2 2.7 %fusion.86 = f32[1,256,512]{2,1,0:T(8,128)} fusion(bf16[256,512]{1,0:T(8,128)(2,1)} %reduce-scatter.5.cloned.1.call-done, s32[1,256,512]{2,1,0:T(8,128)S(1)} %copy-done.5, f32[512]{0:T(512)S(1)} %bitcast.165, f32[512]{0:T(512)S(1)} %bitcast.163), kind=kLoop, calls=%fused_computation.129 | loop fusion | flops 5111808 | bytes 1314816 | tf_op jit(solution)/shard_map/broadcast_in_dim | solution.py:138
  146.9 35.3 %reduce-scatter.3.cloned.1.call-done = bf16[2,512,256]{2,1,0:T(8,128)(2,1)} async-done(((bf16[2,2048,256]{2,1,0:T(8,128)(2,1)}), bf16[2,512,256]{2,1,0:T(8,128)(2,1)}) %reduce-scatter.3.cloned.1.call-update) | async-done | bytes 524304 | tf_op jit(solution)/shard_map/reduce_scatter | solution.py:122
  182.2 3.9 %fusion.33 = f32[1,2,512,256]{3,2,1,0:T(8,128)} fusion(bf16[2,512,256]{2,1,0:T(8,128)(2,1)} %reduce-scatter.3.cloned.1.call-done, s32[1,2,512,256]{3,2,1,0:T(8,128)S(1)} %copy-done.1, f32[2,512]{1,0:T(2,128)S(1)} %get-tuple-element.15, f32[2,512]{1,0:T(2,128)S(1)} %get-tuple-element.14), kind=kLoop, calls=%fused_computation.54 | loop fusion | flops 10223616 | bytes 2629632 | tf_op jit(solution)/shard_map/broadcast_in_dim | solution.py:138
  186.1 2.1 %copy.30 = bf16[1,192,2048]{2,1,0:T(8,128)(2,1)} copy(bf16[1,192,2048]{2,1,0:T(8,128)(2,1)} %bitcast.12) | data formatting | bytes 1572864
  188.2 0.9 copy.31
  (28 shorter events, 0.1 us)
Async XLA Ops:
  7.2 4.3 %copy-start.13 = (f32[1,2,2,512,1]{3,4,2,1,0:T(1,128)S(1)}, f32[1,2,2,512,1]{3,4,2,1,0:T(1,128)}, u32[]{:S(2)}) copy-start(f32[1,2,2,512,1]{3,4,2,1,0:T(1,128)} %param.19) | copy-start | bytes 24580
  7.2 4.4 %copy-start.1 = (s32[1,2,512,256]{3,2,1,0:T(8,128)S(1)}, s32[1,2,512,256]{3,2,1,0:T(8,128)}, u32[]{:S(2)}) copy-start(s32[1,2,512,256]{3,2,1,0:T(8,128)} %param.17) | copy-start | bytes 3145732
  7.2 33.6 %all-gather.5.cloned.1.call-start = ((), (), s32[]{:S(2)}) async-start(), calls=%async_computation.3 | async-start | bytes 1310720 | tf_op jit(solution)/shard_map/all_gather | solution.py:16
  11.4 67.0 %all-gather.3.cloned.1.call-start = ((), (), s32[]{:S(2)}) async-start(), calls=%async_computation.2 | async-start | bytes 2621440 | tf_op jit(solution)/shard_map/all_gather | solution.py:80
  11.5 3.9 %copy-start.2 = (bf16[1,192,2048]{2,1,0:T(8,128)(2,1)S(1)}, bf16[1,192,2048]{2,1,0:T(8,128)(2,1)}, u32[]{:S(2)}) copy-start(bf16[1,192,2048]{2,1,0:T(8,128)(2,1)} %param.11) | copy-start | bytes 2359300
  11.5 4.2 %copy-start = (bf16[1,192,2048]{2,1,0:T(8,128)(2,1)S(1)}, bf16[1,192,2048]{2,1,0:T(8,128)(2,1)}, u32[]{:S(2)}) copy-start(bf16[1,192,2048]{2,1,0:T(8,128)(2,1)} %param.12) | copy-start | bytes 2359300
  15.4 96.3 %all-reduce.3.cloned.1.call-start = ((), (), s32[]{:S(2)}) async-start(), calls=%async_computation.6 | async-start | bytes 3145728 | tf_op jit(solution)/shard_map/psum | solution.py:102
  15.7 62.7 %copy-start.12 = (f32[1,2048]{1,0:T(1,128)S(1)}, f32[1,2048]{1,0:T(1,128)}, u32[]{:S(2)}) copy-start(f32[1,2048]{1,0:T(1,128)} %param.14) | copy-start | bytes 24580
  78.4 1.9 copy-start.6
  80.4 2.6 %copy-start.9 = (f32[192,256]{1,0:T(8,128)}, f32[192,256]{1,0:T(8,128)S(1)}, u32[]{:S(2)}) copy-start(f32[192,256]{1,0:T(8,128)S(1)} %fusion.43) | copy-start | bytes 589828
  80.4 1.2 copy-start.3
  80.4 1.6 copy-start.8
  80.8 2.2 %copy-start.10 = (f32[192,256]{1,0:T(8,128)}, f32[192,256]{1,0:T(8,128)S(1)}, u32[]{:S(2)}) copy-start(f32[192,256]{1,0:T(8,128)S(1)} %fusion.45) | copy-start | bytes 589828
  87.8 2.0 copy-start.7
  91.1 53.1 %reduce-scatter.5.cloned.1.call-start = ((), (), s32[]{:S(2)}) async-start(), calls=%async_computation.5 | async-start | bytes 1310720 | tf_op jit(solution)/shard_map/reduce_scatter | solution.py:125
  93.7 88.6 %reduce-scatter.3.cloned.1.call-start = ((), (), s32[]{:S(2)}) async-start(), calls=%async_computation.4 | async-start | bytes 2621440 | tf_op jit(solution)/shard_map/reduce_scatter | solution.py:122
  93.7 0.9 copy-start.11
  111.7 6.9 %copy-start.4 = (bf16[192,2048]{1,0:T(8,128)(2,1)S(1)}, bf16[192,2048]{1,0:T(8,128)(2,1)}, u32[]{:S(2)}) copy-start(bf16[192,2048]{1,0:T(8,128)(2,1)} %get-tuple-element.5) | copy-start | bytes 2359300
  114.1 32.8 %collective-permute-start = (bf16[192,2048]{1,0:T(8,128)(2,1)}, bf16[192,2048]{1,0:T(8,128)(2,1)}, u32[]{:S(2)}, u32[]{:S(2)}) collective-permute-start(bf16[192,2048]{1,0:T(8,128)(2,1)} %fusion.10), channel_id=1, source_target_pairs={{0,8},{8,16},{16,24},{1,9},{9,17},{17,25},{2,10},{10,18},{18,26},{... | collective-permute-start | bytes 2359304 | tf_op jit(solution)/shard_map/ppermute | solution.py:23
  119.0 25.2 %copy-start.5 = (s32[1,256,512]{2,1,0:T(8,128)S(1)}, s32[1,256,512]{2,1,0:T(8,128)}, u32[]{:S(2)}) copy-start(s32[1,256,512]{2,1,0:T(8,128)} %param.18) | copy-start | bytes 1572868
  120.5 26.4 %collective-permute-start.1 = (bf16[192,2048]{1,0:T(8,128)(2,1)}, bf16[192,2048]{1,0:T(8,128)(2,1)S(1)}, u32[]{:S(2)}, u32[]{:S(2)}) collective-permute-start(bf16[192,2048]{1,0:T(8,128)(2,1)} %fusion.16), channel_id=1, source_target_pairs={{8,0},{16,8},{24,16},{9,1},{17,9},{25,17},{10,2},{18,10},{26,18},{... | collective-permute-start | bytes 2359304 | tf_op jit(solution)/shard_map/ppermute | solution.py:23
Sparse Core Ops, SparseCore 0:
  11.6 29.2 all-gather.4
  43.2 35.1 all-gather.2
  91.3 20.4 all-reduce.2
  115.0 29.1 reduce-scatter.4
  147.0 35.1 reduce-scatter.2
